TPU v7x, 32 devices: a whole 2x2x4 slice. The times are simulated.
32 devices in a mesh: box: 4 (over y, core), dir: 8 (over z, x).
Axes of the slice: x: 2, y: 2, z: 4, core: 2. Of those that a mesh axis runs over, the one named last changes fastest.
Arguments:
- currents: bfloat16 [256, 2, 256, 128], P(('box', 'dir')), may hold values from -6 to 6
- near_blocks: bfloat16 [256, 3, 2, 256, 256], P(('box', 'dir')), may hold values from -0.21875 to 0.21875
- near_mask: int32 [2, 256], replicated, may hold values 0 or 1
- aggregate: bfloat16 [2, 512, 256], replicated, may hold values from -0.375 to 0.375
- disaggregate: bfloat16 [2, 256, 512], replicated, may hold values from -0.25 to 0.25
- centers: float32 [3, 256], replicated, may hold values from 0 to 16
Outputs:
- fields: bfloat16 [256, 2, 256, 128], P(('box', 'dir'))
All inputs are finite; a program needn't handle non-finite values.
Results may differ from a plain program's by a relative error of at most 0.0054.
Values may be sent and summed in bfloat16 or wider, within the bound.
No kernel may reach another device: no remote copies, remote signals or barrier semaphores. Data moves between devices by JAX's collectives and lax.ppermute only.
A program may use at most 64 MiB of HBM per device.

v0:
```python
import math
import jax
import jax.numpy as jnp
from jax import lax
from jax.sharding import PartitionSpec as P

wave_number = 2.0
far_gain = 8.0
golden_turn = 2.399963229728653


def extended(block, sides, width):
    for axis, dim in sides:
        count = lax.axis_size(axis)
        forward = [(i, i + 1) for i in range(count - 1)]
        backward = [(target, source) for source, target in forward]
        low = lax.ppermute(
            lax.slice_in_dim(block, block.shape[dim] - width, None, axis=dim), axis, forward
        )
        high = lax.ppermute(lax.slice_in_dim(block, 0, width, axis=dim), axis, backward)
        block = jnp.concatenate([low, block, high], axis=dim)
    return block


def direction_cosines(count, first, many):
    order = (first + jnp.arange(many, dtype=jnp.int32)).astype(jnp.float32)
    height = 1.0 - (2.0 * order + 1.0) / count
    radial = jnp.sqrt(1.0 - height * height)
    azimuth = order * golden_turn
    return (radial * jnp.cos(azimuth), radial * jnp.sin(azimuth), height)


def phase_angles(points, first, many, count):
    dir_x, dir_y, dir_z = direction_cosines(count, first, many)
    return wave_number * (
        points[0][:, None] * dir_x[None, :]
        + points[1][:, None] * dir_y[None, :]
        + points[2][:, None] * dir_z[None, :]
    )


def far_matrix(centers, near_mask):
    total_boxes = centers.shape[1]
    squared = jnp.zeros((total_boxes, total_boxes), jnp.float32)
    for axis_number in range(3):
        spread = centers[axis_number][:, None] - centers[axis_number][None, :]
        squared = squared + spread * spread
    spacing = jnp.sqrt(1.0 + squared)
    kernel = jnp.cos(wave_number * spacing) / (1.0 + spacing) * (far_gain / math.sqrt(total_boxes))
    rows = jnp.arange(total_boxes, dtype=jnp.int32)[:, None]
    cols = jnp.arange(total_boxes, dtype=jnp.int32)[None, :]
    linked = (
        (cols == rows)
        | (cols == rows - 1) & (near_mask[0][:, None] == 1)
        | (cols == rows + 1) & (near_mask[1][:, None] == 1)
    )
    return jnp.where(linked, 0.0, kernel).astype(jnp.bfloat16)


def near_field(currents, near_blocks, own_mask):
    padded = extended(currents, ((("box", "dir"), 0),), 1)
    left_on = own_mask[0].astype(jnp.bfloat16)[:, None, None, None]
    right_on = own_mask[1].astype(jnp.bfloat16)[:, None, None, None]
    stacked = jnp.stack([currents, padded[:-2] * left_on, padded[2:] * right_on], 1)

    def product(left, right):
        return jnp.einsum("bjuv,bjva->bua", left, right, preferred_element_type=jnp.float32)

    block_re = near_blocks[:, :, 0]
    block_im = near_blocks[:, :, 1]
    near_re = product(block_re, stacked[:, :, 0]) - product(block_im, stacked[:, :, 1])
    near_im = product(block_re, stacked[:, :, 1]) + product(block_im, stacked[:, :, 0])
    return jnp.stack([near_re, near_im], 1)


def local(currents, near_blocks, near_mask, aggregate, disaggregate, centers):
    device_index = lax.axis_index(("box", "dir"))
    devices = lax.axis_size(("box", "dir"))
    box_count = currents.shape[0]
    total_boxes = centers.shape[1]
    dir_count = aggregate.shape[1]
    dir_share = dir_count // devices
    angle_count = currents.shape[3]
    own_centers = lax.dynamic_slice_in_dim(centers, device_index * box_count, box_count, 1)
    own_mask = lax.dynamic_slice_in_dim(near_mask, device_index * box_count, box_count, 1)
    near = near_field(currents, near_blocks, own_mask)

    def gather_in(matrix, vectors):
        return jnp.einsum("ku,bua->bka", matrix, vectors, preferred_element_type=jnp.float32)

    pat_re = gather_in(aggregate[0], currents[:, 0]) - gather_in(aggregate[1], currents[:, 1])
    pat_im = gather_in(aggregate[0], currents[:, 1]) + gather_in(aggregate[1], currents[:, 0])
    theta = phase_angles(own_centers, 0, dir_count, dir_count)
    cosine = jnp.cos(theta)[:, :, None]
    sine = jnp.sin(theta)[:, :, None]
    pattern = jnp.stack(
        [cosine * pat_re + sine * pat_im, cosine * pat_im - sine * pat_re], 2
    ).astype(jnp.bfloat16)
    arrived = lax.all_to_all(pattern[None], ("box", "dir"), split_axis=2, concat_axis=0, tiled=True)
    flat_pattern = arrived.reshape(total_boxes, dir_share * 2 * angle_count)
    translate = far_matrix(centers, near_mask)
    summed = jnp.dot(translate, flat_pattern, preferred_element_type=jnp.float32).reshape(
        total_boxes, dir_share, 2, angle_count
    )
    theta_all = phase_angles(centers, device_index * dir_share, dir_share, dir_count)
    cos_all = jnp.cos(theta_all)[:, :, None]
    sin_all = jnp.sin(theta_all)[:, :, None]
    sum_re = summed[:, :, 0]
    sum_im = summed[:, :, 1]
    received = jnp.stack(
        [cos_all * sum_re - sin_all * sum_im, cos_all * sum_im + sin_all * sum_re], 2
    ).astype(jnp.bfloat16)
    shaped_back = received.reshape(devices, box_count, dir_share, 2, angle_count)
    returned = lax.all_to_all(shaped_back, ("box", "dir"), split_axis=0, concat_axis=2, tiled=True)
    returned = returned.reshape(box_count, dir_count, 2, angle_count)

    def spread_out(matrix, vectors):
        return jnp.einsum("uk,bka->bua", matrix, vectors, preferred_element_type=jnp.float32)

    far_re = spread_out(disaggregate[0], returned[:, :, 0]) - spread_out(
        disaggregate[1], returned[:, :, 1]
    )
    far_im = spread_out(disaggregate[0], returned[:, :, 1]) + spread_out(
        disaggregate[1], returned[:, :, 0]
    )
    far = jnp.stack([far_re, far_im], 1)
    return (near + far).astype(jnp.bfloat16)


def solution(mesh):
    return jax.shard_map(
        local,
        mesh=mesh,
        in_specs=(
            P(("box", "dir"), None, None, None),
            P(("box", "dir"), None, None, None, None),
            P(),
            P(),
            P(),
            P(),
        ),
        out_specs=P(("box", "dir"), None, None, None),
        check_vma=False,
    )
```

profile of v0, /device:TPU:17, one launch (start us, length us, event | category | flops | bytes accessed | tf_op | source)
XLA Modules:
  0.0 152.9 jit_solution(14616655353102153419)
XLA Ops:
  0.1 1.5 %copy.35 = bf16[8,2,256,128]{2,3,0,1:T(8,128)(2,1)S(1)} copy(bf16[8,2,256,128]{3,2,1,0:T(8,128)(2,1)} %param.6) | data formatting | bytes 2097152 | tf_op args[0]
  1.6 1.8 %fusion.50 = f32[8,128,512]{2,1,0:T(8,128)} fusion(bf16[8,2,256,128]{2,3,0,1:T(8,128)(2,1)S(1)} %copy.35, bf16[2,512,256]{2,1,0:T(8,128)(2,1)S(1)} %copy-done), kind=kOutput, calls=%fused_computation.54 | convolution fusion | flops 268435456 | bytes 2883584 | tf_op jit(solution)/shard_map/ku,bua->bka/dot_general | solution.py:89
  4.2 2.2 %convolution_add_fusion = f32[8,128,512]{2,1,0:T(8,128)S(1)} fusion(f32[8,128,512]{2,1,0:T(8,128)} %fusion.50, bf16[8,2,256,128]{2,3,0,1:T(8,128)(2,1)S(1)} %copy.35, bf16[2,512,256]{2,1,0:T(8,128)(2,1)} %param.9), kind=kOutput, calls=%fused_computation.21 | convolution fusion | flops 268959744 | bytes 4980736 | tf_op jit(solution)/shard_map/ku,bua->bka/dot_general | solution.py:89
  6.6 0.8 fusion.39
  7.6 3.1 %copy.44 = bf16[1,8,512,2,128]{4,1,3,0,2:T(8,128)(2,1)} copy(bf16[1,8,512,2,128]{2,4,1,3,0:T(8,128)(2,1)S(1)} %pad_maximum_fusion.1) | data formatting | bytes 4194304 | tf_op jit(solution)/shard_map/stack | solution.py:96
  10.7 6.2 %all-to-all-start = ((bf16[1,8,512,2,128]{4,1,3,0,2:T(8,128)(2,1)}), bf16[1,8,512,2,128]{4,1,3,0,2:T(8,128)(2,1)S(1)}, u32[]{:S(2)}, u32[]{:S(2)}) async-start(bf16[1,8,512,2,128]{4,1,3,0,2:T(8,128)(2,1)} %copy.44), calls=%async_computation | async-start | bytes 4194304 | tf_op jit(solution)/shard_map/all_to_all | solution.py:99
  17.2 44.8 %all-to-all-done = bf16[1,8,512,2,128]{4,1,3,0,2:T(8,128)(2,1)S(1)} async-done(((bf16[1,8,512,2,128]{4,1,3,0,2:T(8,128)(2,1)}), bf16[1,8,512,2,128]{4,1,3,0,2:T(8,128)(2,1)S(1)}, u32[]{:S(2)}, u32[]{:S(2)}) %all-to-all-start) | async-done | bytes 2097184 | tf_op jit(solution)/shard_map/all_to_all | solution.py:99
  62.5 3.2 %copy.46 = bf16[32,1,8,16,2,128]{5,4,3,2,0,1:T(2,128)(2,1)S(1)} copy(bf16[32,1,8,16,2,128]{5,3,0,4,2,1:T(8,128)(2,1)S(1)} %bitcast.191) | data formatting | bytes 4194304 | tf_op jit(solution)/shard_map/all_to_all | solution.py:99
  65.7 2.8 %reshape.499 = bf16[256,4096]{1,0:T(8,128)(2,1)} reshape(bf16[32,1,8,16,2,128]{5,4,3,2,0,1:T(2,128)(2,1)S(1)} %copy.46) | data formatting | bytes 4194304 | tf_op jit(solution)/shard_map/reshape | solution.py:100
  68.6 3.3 %copy.47 = bf16[4096,256]{1,0:T(8,128)(2,1)S(1)} copy(bf16[4096,256]{0,1:T(8,128)(2,1)} %bitcast.192) | data formatting | bytes 4194304 | tf_op jit(solution)/shard_map/dot_general | solution.py:102
  71.8 1.8 %fusion.72 = f32[256,16,2,128]{3,0,2,1:T(8,128)S(1)} fusion(bf16[16,2,128,256]{3,2,1,0:T(8,128)(2,1)S(1)} %bitcast.193, f32[256]{0:T(256)S(1)} %bitcast.199, f32[256]{0:T(256)S(1)} %bitcast.197, f32[256]{0:T(256)S(1)} %bitcast.195, s32[256]{0:T(256)S(1)} %get-tuple-element.29, s32[256]{0:T(256)S(1)} %get-tuple-element.30, ...), kind=kOutput, calls=%fused_computation.80 | convolution fusion | flops 538312704 | bytes 6297088 | tf_op jit(solution)/shard_map/dot_general | solution.py:102
  73.6 1.4 fusion.41
  75.1 1.2 copy.48
  76.3 1.2 copy.49
  77.5 1.5 pad_maximum_fusion.2
  79.0 7.8 %all-to-all-start.1 = ((bf16[32,8,16,2,128]{4,2,3,1,0:T(8,128)(2,1)}), bf16[32,8,16,2,128]{4,2,3,1,0:T(8,128)(2,1)S(1)}, u32[]{:S(2)}, u32[]{:S(2)}) async-start(bf16[32,8,16,2,128]{4,2,3,1,0:T(8,128)(2,1)} %pad_maximum_fusion.2), calls=%async_computation.1 | async-start | bytes 4194304 | tf_op jit(solution)/shard_map/all_to_all | solution.py:114
  86.9 3.1 %collective-permute-start = (bf16[1,2,256,128]{2,3,0,1:T(8,128)(2,1)S(1)}, bf16[1,2,256,128]{2,3,0,1:T(8,128)(2,1)S(1)}, u32[]{:S(2)}, u32[]{:S(2)}) collective-permute-start(bf16[1,2,256,128]{2,3,0,1:T(8,128)(2,1)S(1)} %get-tuple-element.13), channel_id=1, source_target_pairs={{0,1},{1,2},{2,3},{3,4},{4,5},{5,6},{6,7},{7,8},{8,9},{9,10},{10,1... | collective-permute-start | bytes 393224 | tf_op jit(solution)/shard_map/ppermute | solution.py:17
  90.0 3.3 %collective-permute-start.1 = (bf16[1,2,256,128]{2,3,0,1:T(8,128)(2,1)S(1)}, bf16[1,2,256,128]{2,3,0,1:T(8,128)(2,1)S(1)}, u32[]{:S(2)}, u32[]{:S(2)}) collective-permute-start(bf16[1,2,256,128]{2,3,0,1:T(8,128)(2,1)S(1)} %get-tuple-element.14), channel_id=1, source_target_pairs={{1,0},{2,1},{3,2},{4,3},{5,4},{6,5},{7,6},{8,7},{9,8},{10,9},{11,1... | collective-permute-start | bytes 393224 | tf_op jit(solution)/shard_map/ppermute | solution.py:20
  93.4 44.3 %collective-permute-done = bf16[1,2,256,128]{2,3,0,1:T(8,128)(2,1)S(1)} collective-permute-done((bf16[1,2,256,128]{2,3,0,1:T(8,128)(2,1)S(1)}, bf16[1,2,256,128]{2,3,0,1:T(8,128)(2,1)S(1)}, u32[]{:S(2)}, u32[]{:S(2)}) %collective-permute-start) | collective-permute-done | bytes 131104 | tf_op jit(solution)/shard_map/ppermute | solution.py:17
  138.2 3.3 %fusion.13 = f32[8,128,256]{2,1,0:T(8,128)S(1)} fusion(bf16[8,3,2,256,256]{4,3,2,1,0:T(8,128)(2,1)} %param.7, bf16[8,3,2,256,128]{3,4,1,0,2:T(8,128)(2,1)S(1)} %pad_maximum_fusion), kind=kOutput, calls=%fused_computation.25 | convolution fusion | flops 402653184 | bytes 5767168 | tf_op jit(solution)/shard_map/bjuv,bjva->bua/dot_general | solution.py:67
  141.6 1.1 fusion.16
  142.7 2.1 %fusion.36 = f32[8,1,256,128]{2,3,0,1:T(8,128)} fusion(f32[8,128,256]{2,1,0:T(8,128)S(1)} %fusion.13, bf16[8,3,2,256,256]{4,3,2,1,0:T(8,128)(2,1)S(1)} %bitcast.201, bf16[8,3,2,256,128]{3,4,1,0,2:T(8,128)(2,1)S(1)} %pad_maximum_fusion), kind=kOutput, calls=%fused_computation.36 | convolution fusion | flops 402915328 | bytes 6815744 | tf_op jit(solution)/shard_map/bjuv,bjva->bua/dot_general | solution.py:67
  144.8 2.1 %fusion.30 = f32[8,1,256,128]{2,3,0,1:T(8,128)} fusion(f32[8,128,256]{2,1,0:T(8,128)S(1)} %fusion.16, bf16[8,3,2,256,256]{4,3,2,1,0:T(8,128)(2,1)S(1)} %bitcast.201, bf16[8,3,2,256,128]{3,4,1,0,2:T(8,128)(2,1)S(1)} %pad_maximum_fusion), kind=kOutput, calls=%fused_computation.34 | convolution fusion | flops 402915328 | bytes 6815744 | tf_op jit(solution)/shard_map/bjuv,bjva->bua/dot_general | solution.py:67
  151.6 1.3 copy.53
  (50 shorter events, 7.2 us)
Async XLA Ops:
  0.0 1.6 %copy-start = (bf16[2,512,256]{2,1,0:T(8,128)(2,1)S(1)}, bf16[2,512,256]{2,1,0:T(8,128)(2,1)}, u32[]{:S(2)}) copy-start(bf16[2,512,256]{2,1,0:T(8,128)(2,1)} %param.9) | copy-start | bytes 1572868
  1.6 1.8 %copy-start.1 = (bf16[2,512,256]{2,1,0:T(8,128)(2,1)S(1)}, bf16[2,512,256]{2,1,0:T(8,128)(2,1)}, u32[]{:S(2)}) copy-start(bf16[2,512,256]{2,1,0:T(8,128)(2,1)} %param.9) | copy-start | bytes 1572868
  3.4 0.7 copy-start.7
  4.2 2.4 %copy-start.2 = (bf16[2,512,256]{2,1,0:T(8,128)(2,1)S(1)}, bf16[2,512,256]{2,1,0:T(8,128)(2,1)}, u32[]{:S(2)}) copy-start(bf16[2,512,256]{2,1,0:T(8,128)(2,1)} %param.9) | copy-start | bytes 1572868
  10.7 6.3 %copy-start.8 = (s32[2,256]{1,0:T(2,128)S(1)}, s32[2,256]{1,0:T(2,128)}, u32[]{:S(2)}) copy-start(s32[2,256]{1,0:T(2,128)} %param.8) | copy-start | bytes 6148
  10.7 51.3 %all-to-all-start = ((bf16[1,8,512,2,128]{4,1,3,0,2:T(8,128)(2,1)}), bf16[1,8,512,2,128]{4,1,3,0,2:T(8,128)(2,1)S(1)}, u32[]{:S(2)}, u32[]{:S(2)}) async-start(bf16[1,8,512,2,128]{4,1,3,0,2:T(8,128)(2,1)} %copy.44), calls=%async_computation | async-start | bytes 4194304 | tf_op jit(solution)/shard_map/all_to_all | solution.py:99
  79.0 68.0 %all-to-all-start.1 = ((bf16[32,8,16,2,128]{4,2,3,1,0:T(8,128)(2,1)}), bf16[32,8,16,2,128]{4,2,3,1,0:T(8,128)(2,1)S(1)}, u32[]{:S(2)}, u32[]{:S(2)}) async-start(bf16[32,8,16,2,128]{4,2,3,1,0:T(8,128)(2,1)} %pad_maximum_fusion.2), calls=%async_computation.1 | async-start | bytes 4194304 | tf_op jit(solution)/shard_map/all_to_all | solution.py:114
  86.9 50.8 %collective-permute-start = (bf16[1,2,256,128]{2,3,0,1:T(8,128)(2,1)S(1)}, bf16[1,2,256,128]{2,3,0,1:T(8,128)(2,1)S(1)}, u32[]{:S(2)}, u32[]{:S(2)}) collective-permute-start(bf16[1,2,256,128]{2,3,0,1:T(8,128)(2,1)S(1)} %get-tuple-element.13), channel_id=1, source_target_pairs={{0,1},{1,2},{2,3},{3,4},{4,5},{5,6},{6,7},{7,8},{8,9},{9,10},{10,1... | collective-permute-start | bytes 393224 | tf_op jit(solution)/shard_map/ppermute | solution.py:17
  90.0 47.7 %collective-permute-start.1 = (bf16[1,2,256,128]{2,3,0,1:T(8,128)(2,1)S(1)}, bf16[1,2,256,128]{2,3,0,1:T(8,128)(2,1)S(1)}, u32[]{:S(2)}, u32[]{:S(2)}) collective-permute-start(bf16[1,2,256,128]{2,3,0,1:T(8,128)(2,1)S(1)} %get-tuple-element.14), channel_id=1, source_target_pairs={{1,0},{2,1},{3,2},{4,3},{5,4},{6,5},{7,6},{8,7},{9,8},{10,9},{11,1... | collective-permute-start | bytes 393224 | tf_op jit(solution)/shard_map/ppermute | solution.py:20
  137.7 3.9 %slice-start = ((s8[6291456]{0:T(1024)(128)(4,1)}), s8[4194304]{0:T(1024)(128)(4,1)S(1)}, s32[]{:S(2)}) async-start(s8[6291456]{0:T(1024)(128)(4,1)} %bitcast.200), calls=%async_computation.2 | async-start | bytes 8388608
  137.9 3.7 %slice-start.1 = ((s8[6291456]{0:T(1024)(128)(4,1)}), s8[2097152]{0:T(1024)(128)(4,1)S(1)}, s32[]{:S(2)}) async-start(s8[6291456]{0:T(1024)(128)(4,1)} %bitcast.200), calls=%async_computation.3 | async-start | bytes 4194304
  147.0 1.0 copy-start.3
  148.0 1.0 copy-start.4
  149.5 1.2 copy-start.5
  149.6 1.5 %copy-start.6 = (f32[8,1,256,128]{2,3,0,1:T(8,128)S(1)}, f32[8,1,256,128]{2,3,0,1:T(8,128)}, u32[]{:S(2)}) copy-start(f32[8,1,256,128]{2,3,0,1:T(8,128)} %fusion.30) | copy-start | bytes 3145732
where the time goes:
time: 153 us
  waiting for transfers between devices  89.1 us (58%)
  local copies, waits for them, and re-layouts  20.7 us (14%)
  starting transfers between devices  20.5 us (13%)
  matrix products  17.7 us (12%)
  other arithmetic  4.68 us (3%)
    all_to_all x1, waiting for transfers between devices, local(): lax.all_to_all(pattern[None], ('box', 'dir'), split_axis=2, concat_axis=0...  44.8 us
    ppermute x1, waiting for transfers between devices, extended(): lax.ppermute(lax.slice_in_dim(block, block.shape[dim] - width, None, axis...  44.3 us
    dot_general x4, matrix products, product(): jnp.einsum('bjuv,bjva->bua', left, right, preferred_element_type=jnp.floa...  8.69 us
    all_to_all x1, starting transfers between devices, local(): lax.all_to_all(shaped_back, ('box', 'dir'), split_axis=0, concat_axis=2,...  7.83 us
    all_to_all x1, starting transfers between devices, local(): lax.all_to_all(pattern[None], ('box', 'dir'), split_axis=2, concat_axis=0...  6.23 us
    dot_general x4, matrix products, gather_in(): jnp.einsum('ku,bua->bka', matrix, vectors, preferred_element_type=jnp.flo...  5.26 us
    all_to_all x2, local copies, waits for them, and re-layouts, local(): lax.all_to_all(pattern[None], ('box', 'dir'), split_axis=2, concat_axis=0...  3.78 us
    unnamed x23, local copies, waits for them, and re-layouts  3.38 us
  transfers between devices with their start and end apart: 4, of which 2 were waited for; matrix products, arithmetic and copies ran while one was open for 6% of the time, Pallas kernels for 0%

commit v1 on v0

--- a/solution.py
+++ b/solution.py
@@ -111,7 +111,19 @@
         [cos_all * sum_re - sin_all * sum_im, cos_all * sum_im + sin_all * sum_re], 2
     ).astype(jnp.bfloat16)
     shaped_back = received.reshape(devices, box_count, dir_share, 2, angle_count)
-    returned = lax.all_to_all(shaped_back, ("box", "dir"), split_axis=0, concat_axis=2, tiled=True)
+
+    def quotas_fill(inputs):
+        return jnp.concatenate(
+            lax.all_to_all(
+                jnp.stack(jnp.split(inputs, lax.axis_size(("box", "dir")), axis=0), axis=0),
+                ("box", "dir"),
+                0,
+                0,
+            ),
+            axis=2,
+        )
+
+    returned = quotas_fill(shaped_back)
     returned = returned.reshape(box_count, dir_count, 2, angle_count)
 
     def spread_out(matrix, vectors):

time: 153 us -> 174 us (1.14)
  other arithmetic: 4.68 us -> 23.4 us
    unnamed x1 -> x32, other arithmetic: 0.01 us -> 19.7 us
    another operation x2 -> x0, local copies, waits for them, and re-layouts: 2.44 us -> none  [local(): jnp.stack([cos_all * sum_re - sin_all * sum_im, cos_all * sum_im + sin_al...]
    unnamed x23 -> x25, local copies, waits for them, and re-layouts: 3.38 us -> 5.25 us
where the time goes in v1:
time: 174 us; the launch traced here: 173 us
  waiting for transfers between devices  89.1 us (51%)
  other arithmetic  23.4 us (13%)
  local copies, waits for them, and re-layouts  21.1 us (12%)
  starting transfers between devices  20.4 us (12%)
  matrix products  18.6 us (11%)
    all_to_all x1, waiting for transfers between devices, local(): lax.all_to_all(pattern[None], ('box', 'dir'), split_axis=2, concat_axis=0...  44.8 us
    ppermute x1, waiting for transfers between devices, extended(): lax.ppermute(lax.slice_in_dim(block, block.shape[dim] - width, None, axis...  44.3 us
    unnamed x32, other arithmetic  19.7 us
    dot_general x4, matrix products, product(): jnp.einsum('bjuv,bjva->bua', left, right, preferred_element_type=jnp.floa...  8.7 us
    all_to_all x1, starting transfers between devices, quotas_fill(): lax.all_to_all(jnp.stack(jnp.split(inputs, lax.axis_size(('box', 'dir')),...  7.83 us
    all_to_all x1, starting transfers between devices, local(): lax.all_to_all(pattern[None], ('box', 'dir'), split_axis=2, concat_axis=0...  6.23 us
    dot_general x4, matrix products, gather_in(): jnp.einsum('ku,bua->bka', matrix, vectors, preferred_element_type=jnp.flo...  5.26 us
    unnamed x25, local copies, waits for them, and re-layouts  5.25 us
  transfers between devices with their start and end apart: 4, of which 2 were waited for; matrix products, arithmetic and copies ran while one was open for 6% of the time, Pallas kernels for 0%

profile of v1, /device:TPU:17, one launch (start us, length us, event | category | flops | bytes accessed | tf_op | source)
XLA Modules:
  0.0 173.0 jit_solution(6356707030455421786)
XLA Ops:
  0.1 1.5 copy.34
  1.6 1.8 %fusion.52 = f32[8,128,512]{2,1,0:T(8,128)} fusion(bf16[8,2,256,128]{2,3,0,1:T(8,128)(2,1)S(1)} %copy.34, bf16[2,512,256]{2,1,0:T(8,128)(2,1)S(1)} %copy-done.1), kind=kOutput, calls=%fused_computation.115 | convolution fusion | flops 268435456 | bytes 2883584 | tf_op jit(solution)/shard_map/ku,bua->bka/dot_general | solution.py:89
  4.2 2.2 %convolution_add_fusion = f32[8,128,512]{2,1,0:T(8,128)S(1)} fusion(f32[8,128,512]{2,1,0:T(8,128)} %fusion.52, bf16[8,2,256,128]{2,3,0,1:T(8,128)(2,1)S(1)} %copy.34, bf16[2,512,256]{2,1,0:T(8,128)(2,1)} %param.9), kind=kOutput, calls=%fused_computation.82 | convolution fusion | flops 268959744 | bytes 4980736 | tf_op jit(solution)/shard_map/ku,bua->bka/dot_general | solution.py:89
  6.6 0.8 fusion.39
  7.6 3.1 %copy.43 = bf16[1,8,512,2,128]{4,1,3,0,2:T(8,128)(2,1)} copy(bf16[1,8,512,2,128]{2,4,1,3,0:T(8,128)(2,1)S(1)} %pad_maximum_fusion.1) | data formatting | bytes 4194304 | tf_op jit(solution)/shard_map/stack | solution.py:96
  10.7 6.2 %all-to-all-start = ((bf16[1,8,512,2,128]{4,1,3,0,2:T(8,128)(2,1)}), bf16[1,8,512,2,128]{4,1,3,0,2:T(8,128)(2,1)S(1)}, u32[]{:S(2)}, u32[]{:S(2)}) async-start(bf16[1,8,512,2,128]{4,1,3,0,2:T(8,128)(2,1)} %copy.43), calls=%async_computation | async-start | bytes 4194304 | tf_op jit(solution)/shard_map/all_to_all | solution.py:99
  17.2 44.8 %all-to-all-done = bf16[1,8,512,2,128]{4,1,3,0,2:T(8,128)(2,1)S(1)} async-done(((bf16[1,8,512,2,128]{4,1,3,0,2:T(8,128)(2,1)}), bf16[1,8,512,2,128]{4,1,3,0,2:T(8,128)(2,1)S(1)}, u32[]{:S(2)}, u32[]{:S(2)}) %all-to-all-start) | async-done | bytes 2097184 | tf_op jit(solution)/shard_map/all_to_all | solution.py:99
  62.5 3.2 %copy.45 = bf16[32,1,8,16,2,128]{5,4,3,2,0,1:T(2,128)(2,1)S(1)} copy(bf16[32,1,8,16,2,128]{5,3,0,4,2,1:T(8,128)(2,1)S(1)} %bitcast.246) | data formatting | bytes 4194304 | tf_op jit(solution)/shard_map/all_to_all | solution.py:99
  65.8 2.8 %reshape.558 = bf16[256,4096]{1,0:T(8,128)(2,1)} reshape(bf16[32,1,8,16,2,128]{5,4,3,2,0,1:T(2,128)(2,1)S(1)} %copy.45) | data formatting | bytes 4194304 | tf_op jit(solution)/shard_map/reshape | solution.py:100
  68.6 3.3 %copy.46 = bf16[4096,256]{1,0:T(8,128)(2,1)S(1)} copy(bf16[4096,256]{0,1:T(8,128)(2,1)} %bitcast.247) | data formatting | bytes 4194304 | tf_op jit(solution)/shard_map/dot_general | solution.py:102
  71.8 1.8 %fusion.74 = f32[256,16,2,128]{3,0,2,1:T(8,128)S(1)} fusion(bf16[16,2,128,256]{3,2,1,0:T(8,128)(2,1)S(1)} %bitcast.248, f32[256]{0:T(256)S(1)} %bitcast.254, f32[256]{0:T(256)S(1)} %bitcast.252, f32[256]{0:T(256)S(1)} %bitcast.250, s32[256]{0:T(256)S(1)} %get-tuple-element.31, s32[256]{0:T(256)S(1)} %get-tuple-element.32, ...), kind=kOutput, calls=%fused_computation.141 | convolution fusion | flops 538312704 | bytes 6297088 | tf_op jit(solution)/shard_map/dot_general | solution.py:102
  73.6 1.4 subtract_convert_fusion
  95.4 7.8 %all-to-all-start.1 = ((bf16[32,1,8,16,2,128]{5,2,4,3,1,0:T(8,128)(2,1)}), bf16[32,1,8,16,2,128]{5,2,4,3,1,0:T(8,128)(2,1)S(1)}, u32[]{:S(2)}, u32[]{:S(2)}) async-start(bf16[32,1,8,16,2,128]{5,2,4,3,1,0:T(8,128)(2,1)} %constant_dynamic-update-slice_fusion), calls=%async_computation.1 | async-start | bytes 4194304 | tf_op jit(solution)/shard_map/all_to_all | solution.py:117
  103.3 3.1 %collective-permute-start = (bf16[1,2,256,128]{2,3,0,1:T(8,128)(2,1)S(1)}, bf16[1,2,256,128]{2,3,0,1:T(8,128)(2,1)S(1)}, u32[]{:S(2)}, u32[]{:S(2)}) collective-permute-start(bf16[1,2,256,128]{2,3,0,1:T(8,128)(2,1)S(1)} %get-tuple-element.15), channel_id=1, source_target_pairs={{0,1},{1,2},{2,3},{3,4},{4,5},{5,6},{6,7},{7,8},{8,9},{9,10},{10,1... | collective-permute-start | bytes 393224 | tf_op jit(solution)/shard_map/ppermute | solution.py:17
  106.4 3.3 %collective-permute-start.1 = (bf16[1,2,256,128]{2,3,0,1:T(8,128)(2,1)S(1)}, bf16[1,2,256,128]{2,3,0,1:T(8,128)(2,1)S(1)}, u32[]{:S(2)}, u32[]{:S(2)}) collective-permute-start(bf16[1,2,256,128]{2,3,0,1:T(8,128)(2,1)S(1)} %get-tuple-element.16), channel_id=1, source_target_pairs={{1,0},{2,1},{3,2},{4,3},{5,4},{6,5},{7,6},{8,7},{9,8},{10,9},{11,1... | collective-permute-start | bytes 393224 | tf_op jit(solution)/shard_map/ppermute | solution.py:20
  109.7 44.3 %collective-permute-done = bf16[1,2,256,128]{2,3,0,1:T(8,128)(2,1)S(1)} collective-permute-done((bf16[1,2,256,128]{2,3,0,1:T(8,128)(2,1)S(1)}, bf16[1,2,256,128]{2,3,0,1:T(8,128)(2,1)S(1)}, u32[]{:S(2)}, u32[]{:S(2)}) %collective-permute-start) | collective-permute-done | bytes 131104 | tf_op jit(solution)/shard_map/ppermute | solution.py:17
  154.6 3.3 %fusion.13 = f32[8,128,256]{2,1,0:T(8,128)S(1)} fusion(bf16[8,3,2,256,256]{4,3,2,1,0:T(8,128)(2,1)} %param.7, bf16[8,3,2,256,128]{3,4,1,0,2:T(8,128)(2,1)S(1)} %pad_maximum_fusion), kind=kOutput, calls=%fused_computation.86 | convolution fusion | flops 402653184 | bytes 5767168 | tf_op jit(solution)/shard_map/bjuv,bjva->bua/dot_general | solution.py:67
  158.0 1.1 fusion.16
  159.1 2.1 %fusion.36 = f32[8,1,256,128]{2,3,0,1:T(8,128)} fusion(f32[8,128,256]{2,1,0:T(8,128)S(1)} %fusion.13, bf16[8,3,2,256,256]{4,3,2,1,0:T(8,128)(2,1)S(1)} %bitcast.256, bf16[8,3,2,256,128]{3,4,1,0,2:T(8,128)(2,1)S(1)} %pad_maximum_fusion), kind=kOutput, calls=%fused_computation.97 | convolution fusion | flops 402915328 | bytes 6815744 | tf_op jit(solution)/shard_map/bjuv,bjva->bua/dot_general | solution.py:67
  161.2 2.1 %fusion.30 = f32[8,1,256,128]{2,3,0,1:T(8,128)} fusion(f32[8,128,256]{2,1,0:T(8,128)S(1)} %fusion.16, bf16[8,3,2,256,256]{4,3,2,1,0:T(8,128)(2,1)S(1)} %bitcast.256, bf16[8,3,2,256,128]{3,4,1,0,2:T(8,128)(2,1)S(1)} %pad_maximum_fusion), kind=kOutput, calls=%fused_computation.95 | convolution fusion | flops 402915328 | bytes 6815744 | tf_op jit(solution)/shard_map/bjuv,bjva->bua/dot_general | solution.py:67
  163.4 1.5 fusion.130
  164.8 1.7 copy.57
  167.3 1.5 fusion.49
  171.7 1.3 copy.49
  (81 shorter events, 26.5 us)
Async XLA Ops:
  0.0 1.6 copy-start.1
  1.6 1.8 %copy-start.2 = (bf16[2,512,256]{2,1,0:T(8,128)(2,1)S(1)}, bf16[2,512,256]{2,1,0:T(8,128)(2,1)}, u32[]{:S(2)}) copy-start(bf16[2,512,256]{2,1,0:T(8,128)(2,1)} %param.9) | copy-start | bytes 1572868
  3.4 0.7 copy-start.7
  4.2 2.4 %copy-start.3 = (bf16[2,512,256]{2,1,0:T(8,128)(2,1)S(1)}, bf16[2,512,256]{2,1,0:T(8,128)(2,1)}, u32[]{:S(2)}) copy-start(bf16[2,512,256]{2,1,0:T(8,128)(2,1)} %param.9) | copy-start | bytes 1572868
  10.7 6.3 %copy-start.8 = (s32[2,256]{1,0:T(2,128)S(1)}, s32[2,256]{1,0:T(2,128)}, u32[]{:S(2)}) copy-start(s32[2,256]{1,0:T(2,128)} %param.8) | copy-start | bytes 6148
  10.7 51.3 %all-to-all-start = ((bf16[1,8,512,2,128]{4,1,3,0,2:T(8,128)(2,1)}), bf16[1,8,512,2,128]{4,1,3,0,2:T(8,128)(2,1)S(1)}, u32[]{:S(2)}, u32[]{:S(2)}) async-start(bf16[1,8,512,2,128]{4,1,3,0,2:T(8,128)(2,1)} %copy.43), calls=%async_computation | async-start | bytes 4194304 | tf_op jit(solution)/shard_map/all_to_all | solution.py:99
  95.4 68.0 %all-to-all-start.1 = ((bf16[32,1,8,16,2,128]{5,2,4,3,1,0:T(8,128)(2,1)}), bf16[32,1,8,16,2,128]{5,2,4,3,1,0:T(8,128)(2,1)S(1)}, u32[]{:S(2)}, u32[]{:S(2)}) async-start(bf16[32,1,8,16,2,128]{5,2,4,3,1,0:T(8,128)(2,1)} %constant_dynamic-update-slice_fusion), calls=%async_computation.1 | async-start | bytes 4194304 | tf_op jit(solution)/shard_map/all_to_all | solution.py:117
  103.3 50.8 %collective-permute-start = (bf16[1,2,256,128]{2,3,0,1:T(8,128)(2,1)S(1)}, bf16[1,2,256,128]{2,3,0,1:T(8,128)(2,1)S(1)}, u32[]{:S(2)}, u32[]{:S(2)}) collective-permute-start(bf16[1,2,256,128]{2,3,0,1:T(8,128)(2,1)S(1)} %get-tuple-element.15), channel_id=1, source_target_pairs={{0,1},{1,2},{2,3},{3,4},{4,5},{5,6},{6,7},{7,8},{8,9},{9,10},{10,1... | collective-permute-start | bytes 393224 | tf_op jit(solution)/shard_map/ppermute | solution.py:17
  106.4 47.7 %collective-permute-start.1 = (bf16[1,2,256,128]{2,3,0,1:T(8,128)(2,1)S(1)}, bf16[1,2,256,128]{2,3,0,1:T(8,128)(2,1)S(1)}, u32[]{:S(2)}, u32[]{:S(2)}) collective-permute-start(bf16[1,2,256,128]{2,3,0,1:T(8,128)(2,1)S(1)} %get-tuple-element.16), channel_id=1, source_target_pairs={{1,0},{2,1},{3,2},{4,3},{5,4},{6,5},{7,6},{8,7},{9,8},{10,9},{11,1... | collective-permute-start | bytes 393224 | tf_op jit(solution)/shard_map/ppermute | solution.py:20
  154.0 3.9 %slice-start = ((s8[6291456]{0:T(1024)(128)(4,1)}), s8[4194304]{0:T(1024)(128)(4,1)S(1)}, s32[]{:S(2)}) async-start(s8[6291456]{0:T(1024)(128)(4,1)} %bitcast.255), calls=%async_computation.2 | async-start | bytes 8388608
  154.3 3.7 %slice-start.1 = ((s8[6291456]{0:T(1024)(128)(4,1)}), s8[2097152]{0:T(1024)(128)(4,1)S(1)}, s32[]{:S(2)}) async-start(s8[6291456]{0:T(1024)(128)(4,1)} %bitcast.255), calls=%async_computation.3 | async-start | bytes 4194304
  164.8 1.7 copy-start
  167.3 1.5 copy-start.4
  169.7 1.2 copy-start.5
  169.7 1.5 copy-start.6
